TPU v7x, 256 devices: a whole 4x4x8 slice. The times are simulated.
256 devices in a mesh: grp: 4 (over x_hi, core), pair: 64 (over y, x_lo, z).
Axes of the slice: x: 4 (x_hi: 2, x_lo: 2; x = x_hi * 2 + x_lo), y: 4, z: 8, core: 2. Of those that a mesh axis runs over, the one named last changes fastest.
Arguments:
- chol: bfloat16 [128, 1024, 1024], P(None, 'pair'), may hold values from -0.1875 to 0.1875
- trial: bfloat16 [1024, 512], replicated, may hold values from -2 to 2
- walkers: float32 [256, 1024, 512], P(('grp', 'pair')), may hold values from -10 to 10
- fields: float32 [256, 128], P('grp'), may hold values from -6 to 6
- weights: float32 [256], P(('grp', 'pair')), may hold values from 0.5 to 5
Outputs:
- new_walkers: float32 [256, 1024, 512], P(('grp', 'pair'))
- half_green: float32 [256, 1024, 512], P(('grp', 'pair'))
- new_weights: float32 [256], P(('grp', 'pair'))
All inputs are finite; a program needn't handle non-finite values.
Results may differ from a plain program's by a relative error of at most 0.012.
The roundings to bfloat16 on the way count: a program that leaves them out, or rounds other values in their place, can miss the bound.
Values may be sent and summed in bfloat16 or wider, within the bound.
No kernel may reach another device: no remote copies, remote signals or barrier semaphores. Data moves between devices by JAX's collectives and lax.ppermute only.
A program may use at most 64 MiB of HBM per device.

v0:
```python
import jax
import jax.numpy as jnp
from jax import lax
from jax.sharding import Mesh
from jax.sharding import PartitionSpec as P

TAYLOR = 4
NS_ITERS = 3
PAIR = ("pair_0", "pair_1", "pair_2")
GRP_PAIR = ("grp_0", "grp_1", "pair_0", "pair_1", "pair_2")
GRP = ("grp_0", "grp_1")


root_step = 0.07


def by_axis(array, axes):
    for axis in axes:
        array = lax.psum(array, axis)
    return array


def newton(inner):
    size = inner.shape[-1]
    entries = jnp.diagonal(inner, axis1=1, axis2=2)
    inverse = jnp.eye(size, dtype=jnp.float32)[None] / entries[:, None, :]
    for sweep in range(NS_ITERS):
        product = jnp.einsum("wij,wjk->wik", inner, inverse, precision=lax.Precision.HIGHEST)
        inverse = 2.0 * inverse - jnp.einsum(
            "wij,wjk->wik", inverse, product, precision=lax.Precision.HIGHEST
        )
    return inverse


def solve_half(trial_wide, orbitals):
    inner = jnp.einsum("mi,wmj->wij", trial_wide, orbitals, precision=lax.Precision.HIGHEST)
    inverse = newton(inner)
    return jnp.einsum("wmi,wij->wmj", orbitals, inverse, precision=lax.Precision.HIGHEST)


def per_device(chol, trial, walkers, fields, weights):
    own_count = walkers.shape[0]
    vectors = chol.shape[0]
    block_rows = chol.shape[1]
    width = chol.shape[2]
    trial_wide = trial.astype(jnp.float32)
    theta = solve_half(trial_wide, walkers).astype(jnp.bfloat16)
    theta_block = lax.all_to_all(theta, PAIR, split_axis=1, concat_axis=0, tiled=True)
    green_block = jnp.einsum(
        "wri,qi->wrq", theta_block, trial, preferred_element_type=jnp.float32
    ).astype(jnp.bfloat16)
    group_count = green_block.shape[0]
    chol_flat = chol.reshape(vectors, block_rows * width)
    partial_bias = lax.dot_general(
        green_block.reshape(group_count, block_rows * width),
        chol_flat,
        (((1,), (1,)), ((), ())),
        preferred_element_type=jnp.float32,
    )
    bias = by_axis(partial_bias, PAIR)
    xbar = -root_step * bias
    shifted = (fields - xbar).astype(jnp.bfloat16)
    op_block = (
        (root_step * jnp.dot(shifted, chol_flat, preferred_element_type=jnp.float32))
        .reshape(group_count, block_rows, width)
        .astype(jnp.bfloat16)
    )
    operator = lax.all_to_all(op_block, PAIR, split_axis=0, concat_axis=1, tiled=True)
    term = walkers
    total = walkers
    for order in range(1, TAYLOR + 1):
        term = jnp.einsum(
            "wpq,wqi->wpi", operator, term.astype(jnp.bfloat16), preferred_element_type=jnp.float32
        ) / float(order)
        total = total + term
    half_green = solve_half(trial_wide, total)
    start = lax.axis_index(PAIR) * own_count
    own_draws = lax.dynamic_slice_in_dim(fields, start, own_count, 0)
    own_xbar = lax.dynamic_slice_in_dim(xbar, start, own_count, 0)
    raw = weights * jnp.exp(jnp.sum(own_draws * own_xbar - 0.5 * own_xbar * own_xbar, axis=1))
    whole = by_axis(jnp.sum(raw), GRP_PAIR)
    count_all = own_count * lax.axis_size(GRP) * lax.axis_size(PAIR)
    new_weights = raw * (count_all / whole)
    return (total, half_green, new_weights)


def solution(mesh):
    torus = Mesh(
        mesh.devices.reshape(2, 2, 4, 2, 8), ("grp_0", "grp_1", "pair_0", "pair_1", "pair_2")
    )
    return jax.shard_map(
        per_device,
        mesh=torus,
        in_specs=(P(None, PAIR, None), P(), P(GRP_PAIR, None, None), P(GRP, None), P(GRP_PAIR)),
        out_specs=(P(GRP_PAIR, None, None), P(GRP_PAIR, None, None), P(GRP_PAIR)),
        check_vma=False,
    )
```

profile of v0, /device:TPU:2, one launch (start us, length us, event | category | flops | bytes accessed | tf_op | source)
XLA Modules:
  0.0 258.7 jit_solution(13848121245290278904)
XLA Ops:
  0.6 0.0 copy-start
  0.7 1.2 copy-done
  1.9 3.4 %fusion.9 = f32[512,512]{1,0:T(8,128)S(1)} fusion(bf16[1024,512]{1,0:T(8,128)(2,1)S(1)} %copy-done, f32[1,1024,512]{2,1,0:T(8,128)} %param.7), kind=kOutput, calls=%fused_computation.16 | convolution fusion | flops 3221225472 | bytes 4194304 | tf_op jit(solution)/shard_map/mi,wmj->wij/dot_general | solution.py:36
  5.3 4.8 %gather_fusion = f32[512]{0:T(512)S(1)} fusion(f32[512,512]{0,1:T(8,128)S(1)} %bitcast.99, s32[512]{0:T(512)S(1)} %bitcast.96), kind=kCustom, calls=%fused_computation | custom fusion | bytes 8192 | tf_op jit(solution)/shard_map/jit(diagonal)/gather | solution.py:25
  10.1 1.8 fusion.40
  11.9 1.8 convolution_subtract_fusion.5
  13.7 1.9 fusion.50
  15.7 1.9 convolution_subtract_fusion.4
  17.5 1.9 fusion.51
  19.4 0.0 copy-start.1
  19.4 1.9 convolution_subtract_fusion.3
  21.3 8.1 %fusion.20 = bf16[1,1024,512]{1,2,0:T(8,128)(2,1)} fusion(f32[512,512]{1,0:T(8,128)S(1)} %convolution_subtract_fusion.3, f32[1,1024,512]{2,1,0:T(8,128)S(1)} %copy-done.1), kind=kOutput, calls=%fused_computation.26 | convolution fusion | flops 3221749760 | bytes 4194304 | tf_op jit(solution)/shard_map/wmi,wij->wmj/dot_general | solution.py:38
  29.4 6.0 %copy.11 = bf16[1,1024,512]{2,0,1:T(2,128)(2,1)} copy(bf16[1,1024,512]{1,2,0:T(8,128)(2,1)} %fusion.20) | data formatting | bytes 2097152 | tf_op jit(solution)/shard_map/convert_element_type | solution.py:47
  35.4 0.5 broadcast.74
  35.9 9.0 %reduce.1 = bf16[1024,512]{1,0:T(8,128)(2,1)} reduce(bf16[1024,1,512]{2,1,0:T(2,128)(2,1)} %bitcast.104, bf16[]{:T(256)} %broadcast.74), dimensions={1}, to_apply=%bitcast.65.reduce_sub_computation | reduce | bytes 2097154
  44.9 2.6 %reshape.206 = bf16[64,2,4096]{2,1,0:T(2,128)(2,1)} reshape(bf16[1024,512]{1,0:T(8,128)(2,1)} %reduce.1) | data formatting | bytes 2097152
  47.5 13.5 %all-to-all-start = ((bf16[64,2,4096]{2,1,0:T(2,128)(2,1)}), bf16[64,2,4096]{2,1,0:T(2,128)(2,1)}, u32[]{:S(2)}, u32[]{:S(2)}) async-start(bf16[64,2,4096]{2,1,0:T(2,128)(2,1)} %reshape.206), calls=%async_computation | async-start | bytes 2097152 | tf_op jit(solution)/shard_map/all_to_all | solution.py:48
  61.0 7.1 %copy.15 = bf16[16,8,16,1024]{3,1,2,0:T(8,128)(2,1)} copy(bf16[16,8,16,1024]{3,2,1,0:T(8,128)(2,1)} %bitcast.105) | data formatting | bytes 8388608
  68.1 20.8 %all-to-all-done = bf16[64,2,4096]{2,1,0:T(2,128)(2,1)} async-done(((bf16[64,2,4096]{2,1,0:T(2,128)(2,1)}), bf16[64,2,4096]{2,1,0:T(2,128)(2,1)}, u32[]{:S(2)}, u32[]{:S(2)}) %all-to-all-start) | async-done | bytes 1048608 | tf_op jit(solution)/shard_map/all_to_all | solution.py:48
  88.9 7.5 %reshape.207 = bf16[1024,1,512]{2,1,0:T(2,128)(2,1)} reshape(bf16[64,2,4096]{2,1,0:T(2,128)(2,1)} %all-to-all-done) | data formatting | bytes 2097152
  96.4 2.8 %copy.14 = bf16[1,1024,512]{2,1,0:T(8,128)(2,1)} copy(bf16[1,1024,512]{2,0,1:T(2,128)(2,1)} %bitcast.102) | data formatting | bytes 2097152
  99.2 9.3 %fusion.23 = f32[64,128]{1,0:T(8,128)S(1)} fusion(bf16[128,16,1024]{2,1,0:T(8,128)(2,1)} %param.5, bf16[1024,512]{1,0:T(8,128)(2,1)S(1)} %copy-done, bf16[64,16,512]{2,1,0:T(8,128)(2,1)} %bitcast.106), kind=kOutput, calls=%fused_computation.33 | convolution fusion | flops 1343225856 | bytes 6324224 | tf_op jit(solution)/shard_map/dot_general | solution.py:54
  108.5 15.9 %psum.56 = f32[64,128]{1,0:T(8,128)S(1)} all-reduce(f32[64,128]{1,0:T(8,128)S(1)} %fusion.23), channel_id=1, replica_groups=mesh['grp_0'=2,'grp_1'=2,'pair_0'=4,'pair_1'=2,'pair_2'=8] {'pair_0'}, use_global_device_ids=true, to_apply=%region_0.1 | all-reduce | flops 8192 | bytes 65536 | tf_op jit(solution)/shard_map/psum | solution.py:19
  124.4 7.9 %psum.57 = f32[64,128]{1,0:T(8,128)S(1)} all-reduce(f32[64,128]{1,0:T(8,128)S(1)} %psum.56), channel_id=1, replica_groups=mesh['grp_0'=2,'grp_1'=2,'pair_0'=4,'pair_1'=2,'pair_2'=8] {'pair_1'}, use_global_device_ids=true, to_apply=%region_1.2 | all-reduce | flops 8192 | bytes 65536 | tf_op jit(solution)/shard_map/psum | solution.py:19
  132.3 28.7 %psum.58 = f32[64,128]{1,0:T(8,128)S(1)} all-reduce(f32[64,128]{1,0:T(8,128)S(1)} %psum.57), channel_id=1, replica_groups=mesh['grp_0'=2,'grp_1'=2,'pair_0'=4,'pair_1'=2,'pair_2'=8] {'pair_2'}, use_global_device_ids=true, to_apply=%region_2.3 | all-reduce | flops 8192 | bytes 65536 | tf_op jit(solution)/shard_map/psum | solution.py:19
  161.0 3.0 %fusion = bf16[64,16384]{1,0:T(8,128)(2,1)S(1)} fusion(bf16[128,16384]{1,0:T(8,128)(2,1)} %bitcast.100, f32[64,128]{1,0:T(8,128)S(1)} %copy-done.4, f32[64,128]{1,0:T(8,128)S(1)} %psum.58), kind=kOutput, calls=%fused_computation.3 | convolution fusion | flops 270557184 | bytes 6356992 | tf_op jit(solution)/shard_map/dot_general | solution.py:64
  163.9 2.5 copy.16
  166.5 7.7 %all-to-all-start.1 = ((bf16[64,16,1024]{2,1,0:T(8,128)(2,1)}), bf16[64,16,1024]{2,1,0:T(8,128)(2,1)}, u32[]{:S(2)}, u32[]{:S(2)}) async-start(bf16[64,16,1024]{2,1,0:T(8,128)(2,1)} %bitcast.103), calls=%async_computation.1 | async-start | bytes 4194304 | tf_op jit(solution)/shard_map/all_to_all | solution.py:68
  174.8 0.6 fusion.47
  176.1 7.7 %psum.59 = f32[]{:T(128)} all-reduce(f32[]{:T(128)} %bitcast.21), channel_id=1, replica_groups=mesh['grp_0'=2,'grp_1'=2,'pair_0'=4,'pair_1'=2,'pair_2'=8] {'grp_0'}, use_global_device_ids=true, to_apply=%region_4.5 | all-reduce | flops 1 | bytes 8 | tf_op jit(solution)/shard_map/psum | solution.py:19
  183.9 3.1 %psum.60 = f32[]{:T(128)} all-reduce(f32[]{:T(128)} %psum.59), channel_id=1, replica_groups=mesh['grp_0'=2,'grp_1'=2,'pair_0'=4,'pair_1'=2,'pair_2'=8] {'grp_1'}, use_global_device_ids=true, to_apply=%region_5.6 | all-reduce | flops 1 | bytes 8 | tf_op jit(solution)/shard_map/psum | solution.py:19
  186.9 11.4 %psum.61 = f32[]{:T(128)} all-reduce(f32[]{:T(128)} %psum.60), channel_id=1, replica_groups=mesh['grp_0'=2,'grp_1'=2,'pair_0'=4,'pair_1'=2,'pair_2'=8] {'pair_0'}, use_global_device_ids=true, to_apply=%region_6.7 | all-reduce | flops 1 | bytes 8 | tf_op jit(solution)/shard_map/psum | solution.py:19
  198.3 5.8 %psum.62 = f32[]{:T(128)} all-reduce(f32[]{:T(128)} %psum.61), channel_id=1, replica_groups=mesh['grp_0'=2,'grp_1'=2,'pair_0'=4,'pair_1'=2,'pair_2'=8] {'pair_1'}, use_global_device_ids=true, to_apply=%region_7.8 | all-reduce | flops 1 | bytes 8 | tf_op jit(solution)/shard_map/psum | solution.py:19
  204.2 17.8 %psum.63 = f32[]{:T(128)} all-reduce(f32[]{:T(128)} %psum.62), channel_id=1, replica_groups=mesh['grp_0'=2,'grp_1'=2,'pair_0'=4,'pair_1'=2,'pair_2'=8] {'pair_2'}, use_global_device_ids=true, to_apply=%region_8.9 | all-reduce | flops 1 | bytes 8 | tf_op jit(solution)/shard_map/psum | solution.py:19
  222.7 2.8 %fusion.29 = f32[1024,512]{1,0:T(8,128)S(1)} fusion(bf16[1024,1024]{1,0:T(8,128)(2,1)} %bitcast.9, f32[1,1024,512]{2,1,0:T(8,128)S(1)} %copy-done.1), kind=kOutput, calls=%fused_computation.35 | convolution fusion | flops 1074266112 | bytes 6291456 | tf_op jit(solution)/shard_map/wpq,wqi->wpi/dot_general | solution.py:72
  225.5 2.8 %fusion.37 = f32[1024,512]{1,0:T(8,128)S(1)} fusion(bf16[1024,1024]{1,0:T(8,128)(2,1)} %bitcast.9, f32[1024,512]{1,0:T(8,128)S(1)} %fusion.29), kind=kOutput, calls=%fused_computation.41 | convolution fusion | flops 1074266112 | bytes 6291456 | tf_op jit(solution)/shard_map/wpq,wqi->wpi/dot_general | solution.py:72
  228.4 2.9 %fusion.28 = f32[1024,512]{1,0:T(8,128)S(1)} fusion(bf16[1024,1024]{1,0:T(8,128)(2,1)} %bitcast.9, f32[1024,512]{1,0:T(8,128)S(1)} %fusion.37), kind=kOutput, calls=%fused_computation.34 | convolution fusion | flops 1074790400 | bytes 6291456 | tf_op jit(solution)/shard_map/wpq,wqi->wpi/dot_general | solution.py:72
  231.2 3.2 %bitcast_add_fusion = f32[1,1024,512]{2,1,0:T(8,128)S(1)} fusion(f32[1,1024,512]{2,1,0:T(8,128)S(1)} %copy-done.1, f32[1024,512]{1,0:T(8,128)S(1)} %fusion.29, f32[1024,512]{1,0:T(8,128)S(1)} %fusion.28, f32[1024,512]{1,0:T(8,128)S(1)} %fusion.37, bf16[1024,1024]{1,0:T(8,128)(2,1)} %bitcast.9), kind=kOutput, calls=%fused_computation.10 | convolution fusion | flops 1078460416 | bytes 12582912 | tf_op jit(solution)/shard_map/wpq,wqi->wpi/dot_general | solution.py:72
  234.4 1.9 fusion.5
  236.3 4.8 %gather_fusion.1 = f32[512]{0:T(512)S(1)} fusion(f32[512,512]{0,1:T(8,128)S(1)} %bitcast.98, s32[512]{0:T(512)S(1)} %bitcast.97), kind=kCustom, calls=%fused_computation.1 | custom fusion | bytes 8192 | tf_op jit(solution)/shard_map/jit(diagonal)/gather | solution.py:25
  241.1 1.8 fusion.41
  243.0 1.8 convolution_subtract_fusion.2
  244.8 1.9 fusion.52
  246.7 1.9 convolution_subtract_fusion.1
  248.6 1.9 fusion.53
  250.5 0.0 copy-start.3
  250.5 1.9 convolution_subtract_fusion
  252.4 4.8 %fusion.14 = f32[1,1024,512]{2,1,0:T(8,128)} fusion(f32[512,512]{1,0:T(8,128)S(1)} %convolution_subtract_fusion, f32[1,1024,512]{2,1,0:T(8,128)S(1)} %copy-done.3), kind=kOutput, calls=%fused_computation.22 | convolution fusion | flops 3221225472 | bytes 5242880 | tf_op jit(solution)/shard_map/wmi,wij->wmj/dot_general | solution.py:38
  (9 shorter events, 0.0 us)
Async XLA Ops:
  0.6 1.2 copy-start
  19.4 1.9 copy-start.1
  47.5 41.3 %all-to-all-start = ((bf16[64,2,4096]{2,1,0:T(2,128)(2,1)}), bf16[64,2,4096]{2,1,0:T(2,128)(2,1)}, u32[]{:S(2)}, u32[]{:S(2)}) async-start(bf16[64,2,4096]{2,1,0:T(2,128)(2,1)} %reshape.206), calls=%async_computation | async-start | bytes 2097152 | tf_op jit(solution)/shard_map/all_to_all | solution.py:48
  99.2 61.8 %copy-start.4 = (f32[64,128]{1,0:T(8,128)S(1)}, f32[64,128]{1,0:T(8,128)}, u32[]{:S(2)}) copy-start(f32[64,128]{1,0:T(8,128)} %param.8) | copy-start | bytes 98308
  166.5 56.2 %all-to-all-start.1 = ((bf16[64,16,1024]{2,1,0:T(8,128)(2,1)}), bf16[64,16,1024]{2,1,0:T(8,128)(2,1)}, u32[]{:S(2)}, u32[]{:S(2)}) async-start(bf16[64,16,1024]{2,1,0:T(8,128)(2,1)} %bitcast.103), calls=%async_computation.1 | async-start | bytes 4194304 | tf_op jit(solution)/shard_map/all_to_all | solution.py:68
  234.4 1.9 copy-start.2
  250.5 1.9 copy-start.3
where the time goes:
time: 262 us; the launch traced here: 259 us
  blocking collectives  98.3 us (38%)
  matrix products  64.5 us (25%)
  local copies, waits for them, and re-layouts  39.8 us (15%)
  starting transfers between devices  21.2 us (8%)
  waiting for transfers between devices  20.8 us (8%)
  other arithmetic  9.63 us (4%)
  between operations  4.53 us (2%)
    psum x8, blocking collectives, by_axis(): array = lax.psum(array, axis)  98.3 us
    unnamed x16, local copies, waits for them, and re-layouts  24.3 us
    all_to_all x1, waiting for transfers between devices, per_device(): lax.all_to_all(theta, PAIR, split_axis=1, concat_axis=0, tiled=True)  20.8 us
    all_to_all x1, starting transfers between devices, per_device(): lax.all_to_all(theta, PAIR, split_axis=1, concat_axis=0, tiled=True)  13.5 us
    dot_general x2, matrix products, solve_half(): jnp.einsum('wmi,wij->wmj', orbitals, inverse, precision=lax.Precision.HIG...  12.9 us
    dot_general x4, matrix products, per_device(): jnp.einsum('wpq,wqi->wpi', operator, term.astype(jnp.bfloat16), preferred...  11.7 us
    dot_general x6, matrix products, newton(): jnp.einsum('wij,wjk->wik', inner, inverse, precision=lax.Precision.HIGHEST)  11.3 us
    dot_general x6, matrix products, newton(): jnp.einsum('wij,wjk->wik', inverse, product, precision=lax.Precision.HIGH...  11.1 us
  transfers between devices with their start and end apart: 2, of which 1 were waited for; matrix products, arithmetic and copies ran while one was open for 3% of the time, Pallas kernels for 0%

commit v1 on v0

v1 whole, which is shorter than its diff:
```python
import functools
import jax
import jax.numpy as jnp
from jax import lax
from jax.experimental import pallas as pl
from jax.experimental.pallas import tpu as pltpu
from jax.sharding import Mesh
from jax.sharding import PartitionSpec as P

TAYLOR = 4
root_step = 0.07
F32, BF16 = jnp.float32, jnp.bfloat16
NN = (((1,), (0,)), ((), ()))
NT = (((1,), (1,)), ((), ()))
TN = (((0,), (0,)), ((), ()))
VM = pltpu.VMEM
STEPS = 4


def mul(a, b, dims=NN):
    return lax.dot_general(a, b, dims, preferred_element_type=F32)


def pieces(x):
    high = x.astype(BF16)
    return high, (x - high.astype(F32)).astype(BF16)


def wide(a, b):
    (ah, al), (bh, bl) = a, b
    return mul(ah, bh) + (mul(ah, bl) + mul(al, bh))


def correction(inner, passes):
    size = inner.shape[0]
    row = lax.broadcasted_iota(jnp.int32, (size, size), 0)
    col = lax.broadcasted_iota(jnp.int32, (size, size), 1)
    on = row == col
    inv = 1.0 / jnp.sum(jnp.where(on, inner, 0.0), axis=0, keepdims=True)
    e1 = jnp.where(on, 1.0, 0.0) - inner * inv
    if passes == 3:
        p1 = pieces(e1)
        e2 = wide(p1, p1)
        p2 = pieces(e2)
        e3 = wide(p1, p2)
        e4 = wide(p2, p2)
        g = e1 + e2 + e3
        return inv, g + e4 + wide(pieces(g), pieces(e4))
    b1 = e1.astype(BF16)
    e2 = mul(b1, b1)
    b2 = e2.astype(BF16)
    e3 = mul(b1, b2)
    e4 = mul(b2, b2)
    g = e1 + e2 + e3
    return inv, g + e4 + mul(g.astype(BF16), e4.astype(BF16))


def apply_inverse(orbitals, inv, f, passes):
    scaled = orbitals * inv
    if passes == 3:
        return scaled + wide(pieces(scaled), pieces(f))
    return scaled + mul(scaled.astype(BF16), f.astype(BF16))


def inner_of(trial, orbitals):
    high, low = pieces(orbitals)
    return mul(trial, high, TN) + mul(trial, low, TN)


def theta_kernel(newton, last, trial, walkers, theta):
    w = walkers[...]
    inv, f = correction(inner_of(trial[...], w), newton)
    theta[...] = apply_inverse(w, inv, f, last).astype(BF16)


def theta_call(trial, walkers, newton=3, last=3):
    m, n = walkers.shape
    return pl.pallas_call(
        functools.partial(theta_kernel, newton, last),
        out_shape=jax.ShapeDtypeStruct((m, n), BF16),
        in_specs=[pl.BlockSpec(memory_space=VM)] * 2,
        out_specs=pl.BlockSpec(memory_space=VM),
        name="theta",
    )(trial, walkers)


def bias_kernel(theta, trial, chol, extra, out, rows, ordered, total):
    walkers, depth, n = theta.shape
    step = pl.program_id(0)

    @pl.when(step == 0)
    def _():
        for c in range(n // 128):
            lanes = pl.ds(c * 128, 128)
            rows[c] = theta[:, :, lanes].astype(F32).reshape(walkers * depth, 128)
        for r in range(depth):
            for c in range(n // 128):
                ordered[r * walkers : (r + 1) * walkers, c * 128 : (c + 1) * 128] = rows[
                    c, pl.ds(r, walkers, stride=depth), :
                ].astype(BF16)
        total[...] = jnp.zeros_like(total)

    green = mul(ordered[...], trial[...], NT).astype(BF16)
    part = total[...]
    for r in range(depth):
        part = part + mul(green[r * walkers : (r + 1) * walkers], chol[r], NT)
    total[...] = part

    @pl.when(step == pl.num_programs(0) - 1)
    def _():
        for c in range(out.shape[0]):
            out[c, :walkers, :] = part
            out[c, walkers:, :] = extra[...]


def bias_call(theta, trial, chol, extra, copies):
    walkers, depth, n = theta.shape
    _, vectors, width = chol.shape
    block = width // STEPS
    return pl.pallas_call(
        bias_kernel,
        grid=(STEPS,),
        out_shape=jax.ShapeDtypeStruct((copies, walkers + 8, vectors), F32),
        in_specs=[
            pl.BlockSpec((walkers, depth, n), lambda q: (0, 0, 0)),
            pl.BlockSpec((block, n), lambda q: (q, 0)),
            pl.BlockSpec((depth, vectors, block), lambda q: (0, 0, q)),
            pl.BlockSpec((8, vectors), lambda q: (0, 0)),
        ],
        out_specs=pl.BlockSpec((copies, walkers + 8, vectors), lambda q: (0, 0, 0)),
        scratch_shapes=[
            VM((n // 128, walkers * depth, 128), F32),
            VM((walkers * depth, n), BF16),
            VM((walkers, vectors), F32),
        ],
        name="bias",
    )(theta, trial, chol, extra)


def spread_kernel(parts, out):
    total = jnp.sum(parts[...], axis=0)
    for c in range(out.shape[0]):
        out[c] = total


def spread_call(parts, copies):
    return pl.pallas_call(
        spread_kernel,
        out_shape=jax.ShapeDtypeStruct((copies,) + parts.shape[1:], F32),
        in_specs=[pl.BlockSpec(memory_space=VM)],
        out_specs=pl.BlockSpec(memory_space=VM),
        name="spread",
    )(parts)


def operator_kernel(parts, fields, chol, operator, summed, rows, shifted):
    walkers = fields.shape[0]
    depth = chol.shape[0]

    @pl.when(pl.program_id(0) == 0)
    def _():
        total = jnp.sum(parts[...], axis=0)
        summed[...] = total
        shifted[...] = (fields[...] + root_step * total[:walkers]).astype(BF16)

    for r in range(depth):
        block = root_step * mul(shifted[...], chol[r])
        for c in range(rows.shape[0]):
            rows[c, pl.ds(r, walkers, stride=depth), :] = block[:, c * 128 : (c + 1) * 128]
    for c in range(rows.shape[0]):
        lanes = pl.ds(c * 128, 128)
        operator[:, :, lanes] = rows[c].astype(BF16).reshape(walkers, depth, 128)


def operator_call(parts, fields, chol):
    walkers = fields.shape[0]
    depth, vectors, width = chol.shape
    block = width // STEPS
    return pl.pallas_call(
        operator_kernel,
        grid=(STEPS,),
        out_shape=(
            jax.ShapeDtypeStruct((walkers, depth, width), BF16),
            jax.ShapeDtypeStruct(parts.shape[1:], F32),
        ),
        in_specs=[
            pl.BlockSpec(parts.shape, lambda q: (0, 0, 0)),
            pl.BlockSpec(fields.shape, lambda q: (0, 0)),
            pl.BlockSpec((depth, vectors, block), lambda q: (0, 0, q)),
        ],
        out_specs=(
            pl.BlockSpec((walkers, depth, block), lambda q: (0, 0, q)),
            pl.BlockSpec(parts.shape[1:], lambda q: (0, 0)),
        ),
        scratch_shapes=[
            VM((block // 128, walkers * depth, 128), F32),
            VM(fields.shape, BF16),
        ],
        name="operator",
    )(parts, fields, chol)


def step_kernel(newton, last, operator, trial, walkers, total, half, now, sem):
    term = walkers[...].astype(BF16)
    full = walkers[...]
    for order in range(1, TAYLOR + 1):
        fresh = mul(operator[...], term) / float(order)
        full = full + fresh
        term = fresh.astype(BF16)
    now[...] = full
    copy = pltpu.make_async_copy(now, total, sem)
    copy.start()
    inv, f = correction(inner_of(trial[...], now[...]), newton)
    half[...] = apply_inverse(now[...], inv, f, last)
    copy.wait()


def step_call(operator, trial, walkers, newton=3, last=3):
    return pl.pallas_call(
        functools.partial(step_kernel, newton, last),
        out_shape=(jax.ShapeDtypeStruct(walkers.shape, F32),) * 2,
        in_specs=[pl.BlockSpec(memory_space=VM)] * 3,
        out_specs=(pl.BlockSpec(memory_space=pl.ANY), pl.BlockSpec(memory_space=VM)),
        scratch_shapes=[VM(walkers.shape, F32), pltpu.SemaphoreType.DMA],
        name="step",
    )(operator, trial, walkers)


PAIR = ("pair_0", "pair_1", "pair_2")
GRP = ("grp_0", "grp_1")
NEAR = ("pair_0", "pair_1")
FAR = ("pair_2",)


def swap(array, axes):
    return lax.all_to_all(array, axes, split_axis=0, concat_axis=0, tiled=True)


def per_device(chol, trial, walkers, fields, weights):
    _, m, n = walkers.shape
    vectors, depth, _ = chol.shape
    group = lax.axis_size(PAIR)
    place = lax.axis_index(PAIR)
    orbitals = walkers[0]
    theta = theta_call(trial, orbitals).reshape(group, depth, n)
    theta_block = swap(theta, PAIR)
    by_row = jnp.transpose(chol, (1, 0, 2))
    row = lax.broadcasted_iota(jnp.int32, (8, vectors), 0)
    lane = lax.broadcasted_iota(jnp.int32, (8, vectors), 1)
    extra = jnp.where((row == 0) & (lane == place), weights[0], 0.0)
    parts = bias_call(theta_block, trial, by_row, extra, lax.axis_size(FAR))
    parts = spread_call(swap(parts, FAR), lax.axis_size(NEAR))
    op_block, summed = operator_call(swap(parts, NEAR), fields, by_row)
    operator = swap(op_block, PAIR).reshape(m, m)
    total, half_green = step_call(operator, trial, orbitals)
    xbar = -root_step * summed[:group]
    growth = jnp.exp(jnp.sum(fields * xbar - 0.5 * xbar * xbar, axis=1))
    whole = jnp.sum(summed[group, :group] * growth)
    for axis in GRP:
        whole = lax.psum(whole, axis)
    raw = weights * lax.dynamic_slice_in_dim(growth, place, 1, 0)
    new_weights = raw * (group * lax.axis_size(GRP) / whole)
    return (total[None], half_green[None], new_weights)


def solution(mesh):
    torus = Mesh(
        mesh.devices.reshape(2, 2, 4, 2, 8), ("grp_0", "grp_1", "pair_0", "pair_1", "pair_2")
    )
    every = GRP + PAIR
    return jax.shard_map(
        per_device,
        mesh=torus,
        in_specs=(P(None, PAIR, None), P(), P(every, None, None), P(GRP, None), P(every)),
        out_specs=(P(every, None, None), P(every, None, None), P(every)),
        check_vma=False,
    )
```

time: 262 us -> 165 us (0.63)
  the two profiles are of different devices: /device:TPU:2 before, /device:TPU:32 now
where the time goes in v1:
time: 165 us
  waiting for transfers between devices  55.8 us (34%)
  Pallas kernels  39.6 us (24%)
  blocking collectives  35.9 us (22%)
  starting transfers between devices  18.6 us (11%)
  local copies, waits for them, and re-layouts  9.34 us (6%)
  between operations  3.84 us (2%)
    all_to_all x2, waiting for transfers between devices, swap(): return lax.all_to_all(array, axes, split_axis=0, concat_axis=0, tiled=True)  55.8 us
    all_to_all x2, blocking collectives, swap(): return lax.all_to_all(array, axes, split_axis=0, concat_axis=0, tiled=True)  25.7 us
    all_to_all x2, starting transfers between devices, swap(): return lax.all_to_all(array, axes, split_axis=0, concat_axis=0, tiled=True)  18.6 us
    pallas_call x1, Pallas kernels, step_call(): pl.pallas_call(functools.partial(step_kernel, newton, last), out_shape=(j...  14.8 us
    psum x2, blocking collectives, per_device(): whole = lax.psum(whole, axis)  10.2 us
    pallas_call x1, Pallas kernels, theta_call(): pl.pallas_call(functools.partial(theta_kernel, newton, last), out_shape=j...  9.52 us
    unnamed x9, local copies, waits for them, and re-layouts  8.76 us
    pallas_call x1, Pallas kernels, bias_call(): pl.pallas_call(bias_kernel, grid=(STEPS,), out_shape=jax.ShapeDtypeStruct...  8.15 us
  transfers between devices with their start and end apart: 2, of which 2 were waited for; matrix products, arithmetic and copies ran while one was open for 5% of the time, Pallas kernels for 0%

profile of v1, /device:TPU:32, one launch (start us, length us, event | category | flops | bytes accessed | tf_op | source)
XLA Modules:
  0.0 164.5 jit_solution(8786054273111386990)
XLA Ops:
  0.6 9.5 %theta.1 = bf16[1024,512]{1,0:T(8,128)(2,1)} custom-call(bf16[1024,512]{1,0:T(8,128)(2,1)} %trial.5, f32[1024,512]{1,0:T(8,128)} %bitcast.17), custom_call_target="tpu_custom_call" | custom-call | tf_op jit(solution)/shard_map/theta/pallas_call | solution.py:78
  10.1 12.7 %all-to-all-start = ((bf16[64,16,512]{2,1,0:T(8,128)(2,1)}), bf16[64,16,512]{2,1,0:T(8,128)(2,1)S(1)}, u32[]{:S(2)}, u32[]{:S(2)}) async-start(bf16[64,16,512]{2,1,0:T(8,128)(2,1)} %bitcast.20), calls=%async_computation | async-start | bytes 2097152 | tf_op jit(solution)/shard_map/all_to_all | solution.py:236
  23.5 6.4 %copy.10 = bf16[128,16,1024]{2,0,1:T(8,128)(2,1)} copy(bf16[128,16,1024]{2,1,0:T(8,128)(2,1)} %param.5) | data formatting | bytes 8388608 | tf_op args[0]
  29.9 0.7 and_select_fusion.extra
  30.6 21.4 %all-to-all-done.theta = bf16[64,16,512]{2,1,0:T(8,128)(2,1)S(1)} async-done(((bf16[64,16,512]{2,1,0:T(8,128)(2,1)}), bf16[64,16,512]{2,1,0:T(8,128)(2,1)S(1)}, u32[]{:S(2)}, u32[]{:S(2)}) %all-to-all-start) | async-done | bytes 1048608 | tf_op jit(solution)/shard_map/all_to_all | solution.py:236
  52.0 0.0 copy-start.1
  52.1 1.0 copy-done.1
  53.0 8.2 %bias.1 = f32[8,72,128]{2,1,0:T(8,128)} custom-call(bf16[64,16,512]{2,1,0:T(8,128)(2,1)} %copy-done.1, bf16[1024,512]{1,0:T(8,128)(2,1)} %trial.5, bf16[16,128,1024]{2,1,0:T(8,128)(2,1)} %bitcast.15, f32[8,128]{1,0:T(8,128)} %and_select_fusion.extra), custom_call_target="tpu_custom_call" | custom-call | tf_op jit(solution)/shard_map/bias/pallas_call | solution.py:120
  61.2 14.0 %all_to_all.20.parts = f32[8,72,128]{2,1,0:T(8,128)} all-to-all(f32[8,72,128]{2,1,0:T(8,128)} %bias.1), channel_id=1, replica_groups=mesh['grp_0'=2,'grp_1'=2,'pair_0'=4,'pair_1'=2,'pair_2'=8] {'pair_2'}, dimensions={0} | all-to-all | bytes 589824 | tf_op jit(solution)/shard_map/all_to_all | solution.py:236
  75.2 1.7 %spread.1 = f32[8,72,128]{2,1,0:T(8,128)} custom-call(f32[8,72,128]{2,1,0:T(8,128)} %all_to_all.20.parts), custom_call_target="tpu_custom_call" | custom-call | tf_op jit(solution)/shard_map/spread/pallas_call | solution.py:147
  76.9 11.7 %all_to_all.21.parts = f32[8,72,128]{2,1,0:T(8,128)} all-to-all(f32[8,72,128]{2,1,0:T(8,128)} %spread.1), channel_id=1, replica_groups=mesh['grp_0'=2,'grp_1'=2,'pair_0'=4,'pair_1'=2,'pair_2'=8] {'pair_0','pa..., dimensions={0} | all-to-all | bytes 589824 | tf_op jit(solution)/shard_map/all_to_all | solution.py:236
  88.6 5.4 %operator.1 = (bf16[64,16,1024]{2,1,0:T(8,128)(2,1)}, f32[72,128]{1,0:T(8,128)}) custom-call(f32[8,72,128]{2,1,0:T(8,128)} %all_to_all.21.parts, f32[64,128]{1,0:T(8,128)} %fields.1, bf16[16,128,1024]{2,1,0:T(8,128)(2,1)} %bitcast.16), custom_call_target="tpu_custom_call" | custom-call | tf_op jit(solution)/shard_map/operator/pallas_call | solution.py:179
  94.0 0.0 copy-start.2
  94.0 0.0 copy-start.3
  94.0 5.9 %all-to-all-start.3 = ((bf16[64,16,1024]{2,1,0:T(8,128)(2,1)}), bf16[64,16,1024]{2,1,0:T(8,128)(2,1)S(1)}, u32[]{:S(2)}, u32[]{:S(2)}) async-start(bf16[64,16,1024]{2,1,0:T(8,128)(2,1)} %get-tuple-element.7), calls=%async_computation.3 | async-start | bytes 4194304 | tf_op jit(solution)/shard_map/all_to_all | solution.py:236
  99.9 0.0 copy-done.2
  99.9 0.0 copy-done.3
  99.9 0.1 subtract_reduce_fusion
  100.0 0.6 fusion
  100.6 7.0 %psum.14 = f32[]{:T(128)} all-reduce(f32[]{:T(128)} %get-tuple-element.11), channel_id=1, replica_groups=mesh['grp_0'=2,'grp_1'=2,'pair_0'=4,'pair_1'=2,'pair_2'=8] {'grp_0'}, use_global_device_ids=true, to_apply=%region_2.3 | all-reduce | flops 1 | bytes 8 | tf_op jit(solution)/shard_map/psum | solution.py:260
  107.7 3.2 %psum.15 = f32[]{:T(128)} all-reduce(f32[]{:T(128)} %psum.14), channel_id=1, replica_groups=mesh['grp_0'=2,'grp_1'=2,'pair_0'=4,'pair_1'=2,'pair_2'=8] {'grp_1'}, use_global_device_ids=true, to_apply=%region_3.4 | all-reduce | flops 1 | bytes 8 | tf_op jit(solution)/shard_map/psum | solution.py:260
  110.9 0.6 dynamic_slice.3
  112.8 34.4 %all-to-all-done.3 = bf16[64,16,1024]{2,1,0:T(8,128)(2,1)S(1)} async-done(((bf16[64,16,1024]{2,1,0:T(8,128)(2,1)}), bf16[64,16,1024]{2,1,0:T(8,128)(2,1)S(1)}, u32[]{:S(2)}, u32[]{:S(2)}) %all-to-all-start.3) | async-done | bytes 2097184 | tf_op jit(solution)/shard_map/all_to_all | solution.py:236
  147.2 0.0 copy-start
  147.2 1.3 copy-done
  148.6 14.8 %step.1 = (f32[1024,512]{1,0:T(8,128)}, f32[1024,512]{1,0:T(8,128)}) custom-call(bf16[1024,1024]{1,0:T(8,128)(2,1)} %bitcast.19, bf16[1024,512]{1,0:T(8,128)(2,1)} %trial.5, f32[1024,512]{1,0:T(8,128)} %bitcast.18), custom_call_target="tpu_custom_call" | custom-call | tf_op jit(solution)/shard_map/step/pallas_call | solution.py:219
  (2 shorter events, 0.0 us)
Async XLA Ops:
  10.1 41.9 %all-to-all-start = ((bf16[64,16,512]{2,1,0:T(8,128)(2,1)}), bf16[64,16,512]{2,1,0:T(8,128)(2,1)S(1)}, u32[]{:S(2)}, u32[]{:S(2)}) async-start(bf16[64,16,512]{2,1,0:T(8,128)(2,1)} %bitcast.20), calls=%async_computation | async-start | bytes 2097152 | tf_op jit(solution)/shard_map/all_to_all | solution.py:236
  52.0 1.0 copy-start.1
  94.0 5.9 %copy-start.2 = (f32[64,128]{1,0:T(8,128)S(1)}, f32[64,128]{1,0:T(8,128)}, u32[]{:S(2)}) copy-start(f32[64,128]{1,0:T(8,128)} %fields.1) | copy-start | bytes 98308
  94.0 5.9 %copy-start.3 = (f32[72,128]{1,0:T(8,128)S(1)}, f32[72,128]{1,0:T(8,128)}, u32[]{:S(2)}) copy-start(f32[72,128]{1,0:T(8,128)} %get-tuple-element.10) | copy-start | bytes 110596
  94.0 53.2 %all-to-all-start.3 = ((bf16[64,16,1024]{2,1,0:T(8,128)(2,1)}), bf16[64,16,1024]{2,1,0:T(8,128)(2,1)S(1)}, u32[]{:S(2)}, u32[]{:S(2)}) async-start(bf16[64,16,1024]{2,1,0:T(8,128)(2,1)} %get-tuple-element.7), calls=%async_computation.3 | async-start | bytes 4194304 | tf_op jit(solution)/shard_map/all_to_all | solution.py:236
  147.2 1.4 copy-start

commit v2 on v0

v2 whole, which is shorter than its diff:
```python
import functools

import jax
import jax.numpy as jnp
from jax import lax
from jax.experimental import pallas as pl
from jax.experimental.pallas import tpu as pltpu
from jax.sharding import Mesh
from jax.sharding import PartitionSpec as P

TAYLOR = 4
PAIR = ("pair_0", "pair_1", "pair_2")
GRP = ("grp_0", "grp_1")
NEAR = ("pair_0", "pair_1")
FAR = ("pair_2",)
TURN = 2000
PIECES = 4

root_step = 0.07

F32, BF16 = jnp.float32, jnp.bfloat16
NN = (((1,), (0,)), ((), ()))
NT = (((1,), (1,)), ((), ()))
TN = (((0,), (0,)), ((), ()))
VM = pltpu.VMEM
HERE = pl.BlockSpec(memory_space=pltpu.VMEM)
AWAY = pl.BlockSpec(memory_space=pltpu.HBM)


def near(*arrays):
    return [pltpu.with_memory_space_constraint(a, pltpu.VMEM) for a in arrays]


def away(*arrays):
    return [pltpu.with_memory_space_constraint(a, pltpu.HBM) for a in arrays]


def grant(mib):
    return pltpu.CompilerParams(vmem_limit_bytes=mib << 20)


def mul(a, b, dims=NN):
    return lax.dot_general(a, b, dims, preferred_element_type=F32)


def short(a, b):
    return mul(a.astype(BF16), b.astype(BF16))


def inner_of(trial, orbitals):
    high = orbitals.astype(BF16)
    low = (orbitals - high.astype(F32)).astype(BF16)
    return mul(trial, high, TN) + mul(trial, low, TN)


def correction(inner):
    size = inner.shape[0]
    row = lax.broadcasted_iota(jnp.int32, (size, size), 0)
    col = lax.broadcasted_iota(jnp.int32, (size, size), 1)
    on = row == col
    inv = 1.0 / jnp.sum(jnp.where(on, inner, 0.0), axis=0, keepdims=True)
    e1 = jnp.where(on, 1.0, 0.0) - inner * inv
    e2 = short(e1, e1)
    e4 = short(e2, e2)
    g = e1 + e2 + short(e1, e2)
    return inv, g + e4 + short(g, e4)


def theta_kernel(turn, trial_hbm, walkers_hbm, theta, trial, walkers, idle, sems):
    rows = walkers.shape[0] // PIECES
    parts = [pl.ds(c * rows, rows) for c in range(PIECES)]
    copies = []
    for c, part in enumerate(parts):
        copies.append(
            (
                pltpu.make_async_copy(trial_hbm.at[part], trial.at[part], sems.at[0, c]),
                pltpu.make_async_copy(walkers_hbm.at[part], walkers.at[part], sems.at[1, c]),
            )
        )
        for copy in copies[-1]:
            copy.start()
    inner = None
    for c, part in enumerate(parts):
        for copy in copies[c]:
            copy.wait()
        piece = inner_of(trial[part, :], walkers[part, :])
        inner = piece if inner is None else inner + piece
    inv, f = correction(inner)
    scaled = walkers[...] * inv
    theta[...] = (scaled + short(scaled, f)).astype(BF16)
    if TURN:
        idle[...] = jnp.zeros_like(idle)

        def wait(_, carry):
            idle[...] = idle[...] + 1.0
            return carry

        lax.fori_loop(0, turn[0] * TURN, wait, 0)


def theta_call(turn, trial, walkers):
    m, n = walkers.shape
    return pl.pallas_call(
        theta_kernel,
        out_shape=jax.ShapeDtypeStruct((m, n), BF16),
        in_specs=[pl.BlockSpec(memory_space=pltpu.SMEM), AWAY, AWAY],
        out_specs=HERE,
        scratch_shapes=[
            VM(trial.shape, BF16),
            VM(walkers.shape, F32),
            VM((8, 128), F32),
            pltpu.SemaphoreType.DMA((2, PIECES)),
        ],
        compiler_params=grant(24),
        name="theta",
    )(turn, *away(trial, walkers))


def ready_kernel(chol_hbm, trial, flat_hbm, met_hbm, chol, flat, met, loads, stores):
    vectors, depth, width = chol.shape
    n = trial.shape[1]
    some = vectors // PIECES
    copies = []
    for c in range(PIECES):
        part = pl.ds(c * some, some)
        copies.append(pltpu.make_async_copy(chol_hbm.at[part], chol.at[part], loads.at[c]))
        copies[-1].start()
    sent = []
    for c in range(PIECES):
        part = pl.ds(c * some, some)
        copies[c].wait()
        turned = jnp.swapaxes(chol[part], 0, 1)
        for r in range(depth):
            flat[part, r * width : (r + 1) * width] = turned[r]
        sent.append(pltpu.make_async_copy(flat.at[part], flat_hbm.at[part], stores.at[0, c]))
        sent[-1].start()
        product = mul(turned.reshape(depth * some, width), trial[...]).astype(BF16)
        for r in range(depth):
            met[part, r * n : (r + 1) * n] = product[r * some : (r + 1) * some]
        sent.append(pltpu.make_async_copy(met.at[part], met_hbm.at[part], stores.at[1, c]))
        sent[-1].start()
    for copy in sent:
        copy.wait()


def ready_call(chol, trial):
    vectors, depth, width = chol.shape
    n = trial.shape[1]
    return pl.pallas_call(
        ready_kernel,
        out_shape=(
            pltpu.HBM((vectors, depth * width), BF16),
            pltpu.HBM((vectors, depth * n), BF16),
        ),
        in_specs=[AWAY, HERE],
        out_specs=(AWAY, AWAY),
        scratch_shapes=[
            VM(chol.shape, BF16),
            VM((vectors, depth * width), BF16),
            VM((vectors, depth * n), BF16),
            pltpu.SemaphoreType.DMA((PIECES,)),
            pltpu.SemaphoreType.DMA((2, PIECES)),
        ],
        compiler_params=grant(24),
        name="ready",
    )(*away(chol), *near(trial))


def bias_kernel(theta, met_hbm, extra, out, rows, met, sems):
    walkers, depth, n = theta.shape
    some = met.shape[0] // PIECES
    copies = []
    for c in range(PIECES):
        part = pl.ds(c * some, some)
        copies.append(pltpu.make_async_copy(met_hbm.at[part], met.at[part], sems.at[c]))
        copies[-1].start()
    turned = jnp.swapaxes(theta[...], 0, 1)
    for r in range(depth):
        rows[:, r * n : (r + 1) * n] = turned[r]
    for copy in copies:
        copy.wait()
    total = mul(rows[...], met[...], NT).astype(out.dtype)
    for c in range(out.shape[0]):
        out[c, :walkers, :] = total
        out[c, walkers:, :] = extra[...]


def bias_call(theta, met, extra, copies):
    walkers, depth, n = theta.shape
    vectors = met.shape[0]
    return pl.pallas_call(
        bias_kernel,
        out_shape=jax.ShapeDtypeStruct((copies, walkers + extra.shape[0], vectors), extra.dtype),
        in_specs=[HERE, AWAY, HERE],
        out_specs=HERE,
        scratch_shapes=[
            VM((walkers, depth * n), BF16),
            VM(met.shape, BF16),
            pltpu.SemaphoreType.DMA((PIECES,)),
        ],
        compiler_params=grant(16),
        name="bias",
    )(*near(theta), *away(met), *near(extra))


def spread_kernel(parts, out):
    total = jnp.sum(parts[...].astype(F32), axis=0).astype(out.dtype)
    for c in range(out.shape[0]):
        out[c] = total


def spread_call(parts, copies):
    return pl.pallas_call(
        spread_kernel,
        out_shape=jax.ShapeDtypeStruct((copies,) + parts.shape[1:], parts.dtype),
        in_specs=[HERE],
        out_specs=HERE,
        compiler_params=grant(8),
        name="spread",
    )(*near(parts))


def operator_kernel(parts, fields, chol, operator, summed, rows, turned, sems):
    total = jnp.sum(parts[...].astype(F32), axis=0)
    summed[...] = total
    walkers, depth, width = operator.shape
    shifted = (fields[...] + root_step * total[:walkers]).astype(BF16)
    flat = (root_step * mul(shifted, chol[...])).astype(BF16)
    for r in range(depth):
        rows[r] = flat[:, r * width : (r + 1) * width]
    some = walkers // PIECES
    copies = []
    for c in range(PIECES):
        part = pl.ds(c * some, some)
        turned[part] = jnp.swapaxes(rows[:, part, :], 0, 1)
        copies.append(pltpu.make_async_copy(turned.at[part], operator.at[part], sems.at[c]))
        copies[-1].start()
    for copy in copies:
        copy.wait()


def operator_call(parts, fields, chol, depth):
    walkers = fields.shape[0]
    width = chol.shape[1] // depth
    return pl.pallas_call(
        operator_kernel,
        out_shape=(
            pltpu.HBM((walkers, depth, width), BF16),
            jax.ShapeDtypeStruct(parts.shape[1:], F32),
        ),
        in_specs=[HERE] * 3,
        out_specs=(AWAY, HERE),
        scratch_shapes=[
            VM((depth, walkers, width), BF16),
            VM((walkers, depth, width), BF16),
            pltpu.SemaphoreType.DMA((PIECES,)),
        ],
        compiler_params=grant(20),
        name="operator",
    )(*near(parts, fields, chol))


def step_kernel(operator_hbm, trial, walkers, total, half, operator, term, now, done, sems):
    size, n = walkers.shape
    blocks, depth, _ = operator.shape
    some = blocks // PIECES
    rows = size // PIECES
    parts = [pl.ds(c * rows, rows) for c in range(PIECES)]
    copies = []
    for c in range(PIECES):
        part = pl.ds(c * some, some)
        copies.append(
            pltpu.make_async_copy(operator_hbm.at[part], operator.at[part], sems.at[0, c])
        )
        copies[-1].start()
    start = walkers[...].astype(BF16)
    for c, part in enumerate(parts):
        copies[c].wait()
        fresh = mul(operator[c * some : (c + 1) * some].reshape(rows, size), start)
        term[part, :] = fresh.astype(BF16)
        now[part, :] = walkers[part, :] + fresh
    full = now[...]
    last = term[...]
    for order in range(2, TAYLOR + 1):
        fresh = mul(operator[...].reshape(size, size), last) / float(order)
        full = full + fresh
        last = fresh.astype(BF16)
    now[...] = full
    copies = [pltpu.make_async_copy(now, total, sems.at[1, PIECES])]
    copies[0].start()
    inv, f = correction(inner_of(trial[...], now[...]))
    for c, part in enumerate(parts):
        scaled = now[part, :] * inv
        done[part, :] = scaled + short(scaled, f)
        copies.append(pltpu.make_async_copy(done.at[part, :], half.at[part, :], sems.at[1, c]))
        copies[-1].start()
    for copy in copies:
        copy.wait()


def step_call(operator, trial, walkers):
    return pl.pallas_call(
        step_kernel,
        out_shape=(jax.ShapeDtypeStruct(walkers.shape, F32),) * 2,
        in_specs=[AWAY, HERE, HERE],
        out_specs=(AWAY, AWAY),
        scratch_shapes=[
            VM(operator.shape, BF16),
            VM(walkers.shape, BF16),
            VM(walkers.shape, F32),
            VM(walkers.shape, F32),
            pltpu.SemaphoreType.DMA((2, PIECES + 1)),
        ],
        compiler_params=grant(30),
        name="step",
    )(*away(operator), *near(trial, walkers))


def swap(array, axes):
    return lax.all_to_all(array, axes, split_axis=0, concat_axis=0, tiled=True)


def per_device(chol, trial, walkers, fields, weights):
    _, _, n = walkers.shape
    vectors, depth, _ = chol.shape
    group = lax.axis_size(PAIR)
    place = lax.axis_index(PAIR)
    orbitals = walkers[0]
    turn = lax.axis_index("grp_1").astype(jnp.int32).reshape(1)
    theta = theta_call(turn, trial, orbitals).reshape(group, depth, n)
    theta_block = swap(theta, PAIR)
    flat, met = ready_call(chol, trial)
    row = lax.broadcasted_iota(jnp.int32, (16, vectors), 0)
    lane = lax.broadcasted_iota(jnp.int32, (16, vectors), 1)
    weight = weights[0]
    high = lax.reduce_precision(weight, 8, 7)
    middle = lax.reduce_precision(weight - high, 8, 7)
    low = weight - high - middle
    pieces = jnp.where(row == 0, high, jnp.where(row == 1, middle, jnp.where(row == 2, low, 0.0)))
    extra = jnp.where(lane == place, pieces, 0.0).astype(BF16)
    parts = bias_call(theta_block, met, extra, lax.axis_size(FAR))
    parts, later = lax.optimization_barrier((parts, flat))
    parts = spread_call(swap(parts, FAR), lax.axis_size(NEAR))
    op_block, summed = operator_call(swap(parts, NEAR), fields, later, depth)
    operator = swap(op_block, PAIR)
    total, half_green = step_call(operator, trial, orbitals)
    xbar = -root_step * summed[:group]
    growth = jnp.exp(jnp.sum(fields * xbar - 0.5 * xbar * xbar, axis=1))
    whole = jnp.sum(jnp.sum(summed[group:, :group], axis=0) * growth)
    for axis in GRP:
        whole = lax.psum(whole, axis)
    raw = weights * lax.dynamic_slice_in_dim(growth, place, 1, 0)
    new_weights = raw * (group * lax.axis_size(GRP) / whole)
    return (total[None], half_green[None], new_weights)


def solution(mesh):
    torus = Mesh(
        mesh.devices.reshape(2, 2, 4, 2, 8), ("grp_0", "grp_1", "pair_0", "pair_1", "pair_2")
    )
    every = GRP + PAIR
    return jax.shard_map(
        per_device,
        mesh=torus,
        in_specs=(P(None, PAIR, None), P(), P(every, None, None), P(GRP, None), P(every)),
        out_specs=(P(every, None, None), P(every, None, None), P(every)),
        check_vma=False,
    )
```

time: 262 us -> 137 us (0.52)
  the two profiles are of different devices: /device:TPU:2 before, /device:TPU:1 now
where the time goes in v2:
time: 137 us
  Pallas kernels  39.8 us (29%)
  waiting for transfers between devices  38.8 us (28%)
  blocking collectives  29.8 us (22%)
  starting transfers between devices  19.4 us (14%)
  between operations  6.14 us (4%)
  other arithmetic  2.06 us (2%)
    all_to_all x2, waiting for transfers between devices, swap(): return lax.all_to_all(array, axes, split_axis=0, concat_axis=0, tiled=True)  38.8 us
    all_to_all x2, blocking collectives, swap(): return lax.all_to_all(array, axes, split_axis=0, concat_axis=0, tiled=True)  20.2 us
    all_to_all x2, starting transfers between devices, swap(): return lax.all_to_all(array, axes, split_axis=0, concat_axis=0, tiled=True)  19.4 us
    pallas_call x1, Pallas kernels, theta_call(): pl.pallas_call(theta_kernel, out_shape=jax.ShapeDtypeStruct((m, n), BF16)...  19.4 us
    pallas_call x1, Pallas kernels, step_call(): pl.pallas_call(step_kernel, out_shape=(jax.ShapeDtypeStruct(walkers.shape...  10.2 us
    psum x2, blocking collectives, per_device(): whole = lax.psum(whole, axis)  9.6 us
    pallas_call x1, Pallas kernels, ready_call(): pl.pallas_call(ready_kernel, out_shape=(pltpu.HBM((vectors, depth * width...  5.13 us
  transfers between devices with their start and end apart: 2, of which 2 were waited for; matrix products, arithmetic and copies ran while one was open for 2% of the time, Pallas kernels for 4%

profile of v2, /device:TPU:1, one launch (start us, length us, event | category | flops | bytes accessed | tf_op | source)
XLA Modules:
  0.0 136.6 jit_solution(16492768845818448002)
XLA Ops:
  0.6 19.4 %theta.1 = bf16[1024,512]{1,0:T(8,128)(2,1)} custom-call(s32[1]{0:T(128)} %bitcast.turn, bf16[1024,512]{1,0:T(8,128)(2,1)} %trial.3, f32[1024,512]{1,0:T(8,128)} %bitcast.9), custom_call_target="tpu_custom_call" | custom-call | tf_op jit(solution)/shard_map/theta/pallas_call | solution.py:103
  20.0 0.0 copy-start
  20.0 13.7 %all-to-all-start = ((bf16[64,16,512]{2,1,0:T(8,128)(2,1)}), bf16[64,16,512]{2,1,0:T(8,128)(2,1)S(1)}, u32[]{:S(2)}, u32[]{:S(2)}) async-start(bf16[64,16,512]{2,1,0:T(8,128)(2,1)} %bitcast.2), calls=%async_computation | async-start | bytes 2097152 | tf_op jit(solution)/shard_map/all_to_all | solution.py:320
  36.7 0.0 copy-done
  36.7 5.1 %ready.1 = (bf16[128,16384]{1,0:T(8,128)(2,1)}, bf16[128,8192]{1,0:T(8,128)(2,1)}) custom-call(bf16[128,16,1024]{2,1,0:T(8,128)(2,1)} %chol_hbm.1, bf16[1024,512]{1,0:T(8,128)(2,1)S(1)} %copy-done), custom_call_target="tpu_custom_call" | custom-call | tf_op jit(solution)/shard_map/ready/pallas_call | solution.py:149
  41.9 1.3 select_convert_fusion.extra
  43.2 8.5 %all-to-all-done.theta = bf16[64,16,512]{2,1,0:T(8,128)(2,1)S(1)} async-done(((bf16[64,16,512]{2,1,0:T(8,128)(2,1)}), bf16[64,16,512]{2,1,0:T(8,128)(2,1)S(1)}, u32[]{:S(2)}, u32[]{:S(2)}) %all-to-all-start) | async-done | bytes 1048608 | tf_op jit(solution)/shard_map/all_to_all | solution.py:320
  51.7 0.0 copy-start.2
  51.7 0.0 copy-start.3
  51.7 2.5 %bias.1 = bf16[8,80,128]{2,1,0:T(8,128)(2,1)S(1)} custom-call(bf16[64,16,512]{2,1,0:T(8,128)(2,1)S(1)} %all-to-all-done.theta, bf16[128,8192]{1,0:T(8,128)(2,1)} %get-tuple-element.11.met_hbm, bf16[16,128]{1,0:T(8,128)(2,1)S(1)} %select_convert_fusion.extra), custom_call_target="tpu_custom_call" | custom-call | tf_op jit(solution)/shard_map/bias/pallas_call | solution.py:191
  54.3 11.6 %all_to_all.20.parts = bf16[8,80,128]{2,1,0:T(8,128)(2,1)S(1)} all-to-all(bf16[8,80,128]{2,1,0:T(8,128)(2,1)S(1)} %bias.1), channel_id=1, replica_groups=mesh['grp_0'=2,'grp_1'=2,'pair_0'=4,'pair_1'=2,'pair_2'=8] {'pair_2'}, dimensions={0} | all-to-all | bytes 327680 | tf_op jit(solution)/shard_map/all_to_all | solution.py:320
  65.9 8.6 %all_to_all.21.parts = bf16[8,80,128]{2,1,0:T(8,128)(2,1)S(1)} all-to-all(bf16[8,80,128]{2,1,0:T(8,128)(2,1)S(1)} %spread.1), channel_id=1, replica_groups=mesh['grp_0'=2,'grp_1'=2,'pair_0'=4,'pair_1'=2,'pair_2'=8] {'pair_0','pa..., dimensions={0} | all-to-all | bytes 327680 | tf_op jit(solution)/shard_map/all_to_all | solution.py:320
  74.5 0.0 copy-done.2
  74.5 0.0 copy-done.3
  74.5 2.5 %operator.1 = (bf16[64,16,1024]{2,1,0:T(8,128)(2,1)}, f32[80,128]{1,0:T(8,128)S(1)}) custom-call(bf16[8,80,128]{2,1,0:T(8,128)(2,1)S(1)} %all_to_all.21.parts, f32[64,128]{1,0:T(8,128)S(1)} %copy-done.3, bf16[128,16384]{1,0:T(8,128)(2,1)S(1)} %copy-done.2), custom_call_target="tpu_custom_call" | custom-call | tf_op jit(solution)/shard_map/operator/pallas_call | solution.py:245
  77.0 0.0 copy-start.1
  77.0 5.7 %all-to-all-start.3 = ((bf16[64,16,1024]{2,1,0:T(8,128)(2,1)}), bf16[64,16,1024]{2,1,0:T(8,128)(2,1)}, u32[]{:S(2)}, u32[]{:S(2)}) async-start(bf16[64,16,1024]{2,1,0:T(8,128)(2,1)} %get-tuple-element.15), calls=%async_computation.3 | async-start | bytes 4194304 | tf_op jit(solution)/shard_map/all_to_all | solution.py:320
  82.8 0.1 subtract_reduce_fusion
  82.9 0.6 multiply_reduce_fusion
  83.5 6.3 %psum.14 = f32[]{:T(128)} all-reduce(f32[]{:T(128)} %get-tuple-element.19), channel_id=1, replica_groups=mesh['grp_0'=2,'grp_1'=2,'pair_0'=4,'pair_1'=2,'pair_2'=8] {'grp_0'}, use_global_device_ids=true, to_apply=%region_3.4 | all-reduce | flops 1 | bytes 8 | tf_op jit(solution)/shard_map/psum | solution.py:351
  89.8 3.3 %psum.15 = f32[]{:T(128)} all-reduce(f32[]{:T(128)} %psum.14), channel_id=1, replica_groups=mesh['grp_0'=2,'grp_1'=2,'pair_0'=4,'pair_1'=2,'pair_2'=8] {'grp_1'}, use_global_device_ids=true, to_apply=%region_4.5 | all-reduce | flops 1 | bytes 8 | tf_op jit(solution)/shard_map/psum | solution.py:351
  93.1 0.6 dynamic_slice.3
  95.0 30.3 %all-to-all-done.3.operator_hbm = bf16[64,16,1024]{2,1,0:T(8,128)(2,1)} async-done(((bf16[64,16,1024]{2,1,0:T(8,128)(2,1)}), bf16[64,16,1024]{2,1,0:T(8,128)(2,1)}, u32[]{:S(2)}, u32[]{:S(2)}) %all-to-all-start.3) | async-done | bytes 2097184 | tf_op jit(solution)/shard_map/all_to_all | solution.py:320
  125.3 0.0 copy-done.1
  125.3 10.2 %step.1 = (f32[1024,512]{1,0:T(8,128)}, f32[1024,512]{1,0:T(8,128)}) custom-call(bf16[64,16,1024]{2,1,0:T(8,128)(2,1)} %all-to-all-done.3.operator_hbm, bf16[1024,512]{1,0:T(8,128)(2,1)S(1)} %copy-done, f32[1024,512]{1,0:T(8,128)S(1)} %bitcast.10), custom_call_target="tpu_custom_call" | custom-call | tf_op jit(solution)/shard_map/step/pallas_call | solution.py:302
  (5 shorter events, 0.1 us)
Async XLA Ops:
  20.0 16.7 %copy-start = (bf16[1024,512]{1,0:T(8,128)(2,1)S(1)}, bf16[1024,512]{1,0:T(8,128)(2,1)}, u32[]{:S(2)}) copy-start(bf16[1024,512]{1,0:T(8,128)(2,1)} %trial.3) | copy-start | bytes 3145732
  20.0 31.7 %all-to-all-start = ((bf16[64,16,512]{2,1,0:T(8,128)(2,1)}), bf16[64,16,512]{2,1,0:T(8,128)(2,1)S(1)}, u32[]{:S(2)}, u32[]{:S(2)}) async-start(bf16[64,16,512]{2,1,0:T(8,128)(2,1)} %bitcast.2), calls=%async_computation | async-start | bytes 2097152 | tf_op jit(solution)/shard_map/all_to_all | solution.py:320
  51.7 22.8 %copy-start.2 = (bf16[128,16384]{1,0:T(8,128)(2,1)S(1)}, bf16[128,16384]{1,0:T(8,128)(2,1)}, u32[]{:S(2)}) copy-start(bf16[128,16384]{1,0:T(8,128)(2,1)} %get-tuple-element.14.chol) | copy-start | bytes 12582916
  51.7 22.8 %copy-start.3 = (f32[64,128]{1,0:T(8,128)S(1)}, f32[64,128]{1,0:T(8,128)}, u32[]{:S(2)}) copy-start(f32[64,128]{1,0:T(8,128)} %fields.1) | copy-start | bytes 98308
  77.0 48.2 %copy-start.1 = (f32[1,1024,512]{2,1,0:T(8,128)S(1)}, f32[1,1024,512]{2,1,0:T(8,128)}, u32[]{:S(2)}) copy-start(f32[1,1024,512]{2,1,0:T(8,128)} %param.7) | copy-start | bytes 6291460
  77.0 48.2 %all-to-all-start.3 = ((bf16[64,16,1024]{2,1,0:T(8,128)(2,1)}), bf16[64,16,1024]{2,1,0:T(8,128)(2,1)}, u32[]{:S(2)}, u32[]{:S(2)}) async-start(bf16[64,16,1024]{2,1,0:T(8,128)(2,1)} %get-tuple-element.15), calls=%async_computation.3 | async-start | bytes 4194304 | tf_op jit(solution)/shard_map/all_to_all | solution.py:320

commit v3 on v2

--- a/solution.py
+++ b/solution.py
@@ -15,6 +15,7 @@
 FAR = ("pair_2",)
 TURN = 2000
 PIECES = 4
+LOADS = 2
 
 root_step = 0.07
 
@@ -60,9 +61,12 @@
     on = row == col
     inv = 1.0 / jnp.sum(jnp.where(on, inner, 0.0), axis=0, keepdims=True)
     e1 = jnp.where(on, 1.0, 0.0) - inner * inv
-    e2 = short(e1, e1)
-    e4 = short(e2, e2)
-    g = e1 + e2 + short(e1, e2)
+    b1 = e1.astype(BF16)
+    e2 = mul(b1, b1)
+    b2 = e2.astype(BF16)
+    both = mul(jnp.concatenate([b1, b2], axis=0), b2)
+    g = e1 + e2 + both[:size]
+    e4 = both[size:]
     return inv, g + e4 + short(g, e4)
 
 
@@ -225,15 +229,15 @@
     summed[...] = total
     walkers, depth, width = operator.shape
     shifted = (fields[...] + root_step * total[:walkers]).astype(BF16)
-    flat = (root_step * mul(shifted, chol[...])).astype(BF16)
-    for r in range(depth):
-        rows[r] = flat[:, r * width : (r + 1) * width]
-    some = walkers // PIECES
+    some = width // PIECES
     copies = []
     for c in range(PIECES):
         part = pl.ds(c * some, some)
-        turned[part] = jnp.swapaxes(rows[:, part, :], 0, 1)
-        copies.append(pltpu.make_async_copy(turned.at[part], operator.at[part], sems.at[c]))
+        for r in range(depth):
+            start = r * width + c * some
+            rows[r, :, part] = (root_step * mul(shifted, chol[:, start : start + some])).astype(BF16)
+        turned[:, :, part] = jnp.swapaxes(rows[:, :, part], 0, 1)
+        copies.append(pltpu.make_async_copy(turned.at[:, :, part], operator.at[:, :, part], sems.at[c]))
         copies[-1].start()
     for copy in copies:
         copy.wait()
@@ -263,20 +267,22 @@
 def step_kernel(operator_hbm, trial, walkers, total, half, operator, term, now, done, sems):
     size, n = walkers.shape
     blocks, depth, _ = operator.shape
-    some = blocks // PIECES
     rows = size // PIECES
     parts = [pl.ds(c * rows, rows) for c in range(PIECES)]
-    copies = []
-    for c in range(PIECES):
+    some = blocks // LOADS
+    tall = size // LOADS
+    copies = []
+    for c in range(LOADS):
         part = pl.ds(c * some, some)
         copies.append(
             pltpu.make_async_copy(operator_hbm.at[part], operator.at[part], sems.at[0, c])
         )
         copies[-1].start()
     start = walkers[...].astype(BF16)
-    for c, part in enumerate(parts):
+    for c in range(LOADS):
+        part = pl.ds(c * tall, tall)
         copies[c].wait()
-        fresh = mul(operator[c * some : (c + 1) * some].reshape(rows, size), start)
+        fresh = mul(operator[c * some : (c + 1) * some].reshape(tall, size), start)
         term[part, :] = fresh.astype(BF16)
         now[part, :] = walkers[part, :] + fresh
     full = now[...]
@@ -339,9 +345,8 @@
     pieces = jnp.where(row == 0, high, jnp.where(row == 1, middle, jnp.where(row == 2, low, 0.0)))
     extra = jnp.where(lane == place, pieces, 0.0).astype(BF16)
     parts = bias_call(theta_block, met, extra, lax.axis_size(FAR))
-    parts, later = lax.optimization_barrier((parts, flat))
     parts = spread_call(swap(parts, FAR), lax.axis_size(NEAR))
-    op_block, summed = operator_call(swap(parts, NEAR), fields, later, depth)
+    op_block, summed = operator_call(swap(parts, NEAR), fields, flat, depth)
     operator = swap(op_block, PAIR)
     total, half_green = step_call(operator, trial, orbitals)
     xbar = -root_step * summed[:group]

time: 137 us -> 137 us (level)
  no operation moved by 1% of the time
where the time goes in v3:
time: 137 us; the launch traced here: 136 us
  Pallas kernels  39.3 us (29%)
  waiting for transfers between devices  38.8 us (28%)
  blocking collectives  29.8 us (22%)
  starting transfers between devices  19.4 us (14%)
  between operations  6.14 us (4%)
  other arithmetic  2.06 us (2%)
    all_to_all x2, waiting for transfers between devices, swap(): return lax.all_to_all(array, axes, split_axis=0, concat_axis=0, tiled=True)  38.8 us
    all_to_all x2, blocking collectives, swap(): return lax.all_to_all(array, axes, split_axis=0, concat_axis=0, tiled=True)  20.2 us
    all_to_all x2, starting transfers between devices, swap(): return lax.all_to_all(array, axes, split_axis=0, concat_axis=0, tiled=True)  19.4 us
    pallas_call x1, Pallas kernels, theta_call(): pl.pallas_call(theta_kernel, out_shape=jax.ShapeDtypeStruct((m, n), BF16)...  19.4 us
    pallas_call x1, Pallas kernels, step_call(): pl.pallas_call(step_kernel, out_shape=(jax.ShapeDtypeStruct(walkers.shape...  10.1 us
    psum x2, blocking collectives, per_device(): whole = lax.psum(whole, axis)  9.6 us
    pallas_call x1, Pallas kernels, ready_call(): pl.pallas_call(ready_kernel, out_shape=(pltpu.HBM((vectors, depth * width...  5.13 us
  transfers between devices with their start and end apart: 2, of which 2 were waited for; matrix products, arithmetic and copies ran while one was open for 2% of the time, Pallas kernels for 4%

profile of v3, /device:TPU:1, one launch (start us, length us, event | category | flops | bytes accessed | tf_op | source)
XLA Modules:
  0.0 136.1 jit_solution(11547284327895870303)
XLA Ops:
  0.6 19.4 %theta.1 = bf16[1024,512]{1,0:T(8,128)(2,1)} custom-call(s32[1]{0:T(128)} %bitcast.turn, bf16[1024,512]{1,0:T(8,128)(2,1)} %trial.3, f32[1024,512]{1,0:T(8,128)} %bitcast.9), custom_call_target="tpu_custom_call" | custom-call | tf_op jit(solution)/shard_map/theta/pallas_call | solution.py:107
  20.0 0.0 copy-start
  20.0 13.7 %all-to-all-start = ((bf16[64,16,512]{2,1,0:T(8,128)(2,1)}), bf16[64,16,512]{2,1,0:T(8,128)(2,1)S(1)}, u32[]{:S(2)}, u32[]{:S(2)}) async-start(bf16[64,16,512]{2,1,0:T(8,128)(2,1)} %bitcast.2), calls=%async_computation | async-start | bytes 2097152 | tf_op jit(solution)/shard_map/all_to_all | solution.py:326
  36.7 0.0 copy-done
  36.7 5.1 %ready.1 = (bf16[128,16384]{1,0:T(8,128)(2,1)}, bf16[128,8192]{1,0:T(8,128)(2,1)}) custom-call(bf16[128,16,1024]{2,1,0:T(8,128)(2,1)} %chol_hbm.1, bf16[1024,512]{1,0:T(8,128)(2,1)S(1)} %copy-done), custom_call_target="tpu_custom_call" | custom-call | tf_op jit(solution)/shard_map/ready/pallas_call | solution.py:153
  41.9 1.3 select_convert_fusion.extra
  43.2 8.5 %all-to-all-done.theta = bf16[64,16,512]{2,1,0:T(8,128)(2,1)S(1)} async-done(((bf16[64,16,512]{2,1,0:T(8,128)(2,1)}), bf16[64,16,512]{2,1,0:T(8,128)(2,1)S(1)}, u32[]{:S(2)}, u32[]{:S(2)}) %all-to-all-start) | async-done | bytes 1048608 | tf_op jit(solution)/shard_map/all_to_all | solution.py:326
  51.7 0.0 copy-start.2
  51.7 0.0 copy-start.3
  51.7 2.5 %bias.1 = bf16[8,80,128]{2,1,0:T(8,128)(2,1)S(1)} custom-call(bf16[64,16,512]{2,1,0:T(8,128)(2,1)S(1)} %all-to-all-done.theta, bf16[128,8192]{1,0:T(8,128)(2,1)} %get-tuple-element.9.met_hbm, bf16[16,128]{1,0:T(8,128)(2,1)S(1)} %select_convert_fusion.extra), custom_call_target="tpu_custom_call" | custom-call | tf_op jit(solution)/shard_map/bias/pallas_call | solution.py:195
  54.3 11.6 %all_to_all.20.parts = bf16[8,80,128]{2,1,0:T(8,128)(2,1)S(1)} all-to-all(bf16[8,80,128]{2,1,0:T(8,128)(2,1)S(1)} %bias.1), channel_id=1, replica_groups=mesh['grp_0'=2,'grp_1'=2,'pair_0'=4,'pair_1'=2,'pair_2'=8] {'pair_2'}, dimensions={0} | all-to-all | bytes 327680 | tf_op jit(solution)/shard_map/all_to_all | solution.py:326
  65.9 8.6 %all_to_all.21.parts = bf16[8,80,128]{2,1,0:T(8,128)(2,1)S(1)} all-to-all(bf16[8,80,128]{2,1,0:T(8,128)(2,1)S(1)} %spread.1), channel_id=1, replica_groups=mesh['grp_0'=2,'grp_1'=2,'pair_0'=4,'pair_1'=2,'pair_2'=8] {'pair_0','pa..., dimensions={0} | all-to-all | bytes 327680 | tf_op jit(solution)/shard_map/all_to_all | solution.py:326
  74.5 0.0 copy-done.2
  74.5 0.0 copy-done.3
  74.5 2.1 %operator.1 = (bf16[64,16,1024]{2,1,0:T(8,128)(2,1)}, f32[80,128]{1,0:T(8,128)S(1)}) custom-call(bf16[8,80,128]{2,1,0:T(8,128)(2,1)S(1)} %all_to_all.21.parts, f32[64,128]{1,0:T(8,128)S(1)} %copy-done.3, bf16[128,16384]{1,0:T(8,128)(2,1)S(1)} %copy-done.2), custom_call_target="tpu_custom_call" | custom-call | tf_op jit(solution)/shard_map/operator/pallas_call | solution.py:249
  76.7 0.0 copy-start.1
  76.7 5.7 %all-to-all-start.3 = ((bf16[64,16,1024]{2,1,0:T(8,128)(2,1)}), bf16[64,16,1024]{2,1,0:T(8,128)(2,1)}, u32[]{:S(2)}, u32[]{:S(2)}) async-start(bf16[64,16,1024]{2,1,0:T(8,128)(2,1)} %get-tuple-element.11), calls=%async_computation.3 | async-start | bytes 4194304 | tf_op jit(solution)/shard_map/all_to_all | solution.py:326
  82.4 0.1 subtract_reduce_fusion
  82.5 0.6 multiply_reduce_fusion
  83.1 6.3 %psum.14 = f32[]{:T(128)} all-reduce(f32[]{:T(128)} %get-tuple-element.15), channel_id=1, replica_groups=mesh['grp_0'=2,'grp_1'=2,'pair_0'=4,'pair_1'=2,'pair_2'=8] {'grp_0'}, use_global_device_ids=true, to_apply=%region_3.4 | all-reduce | flops 1 | bytes 8 | tf_op jit(solution)/shard_map/psum | solution.py:356
  89.5 3.3 %psum.15 = f32[]{:T(128)} all-reduce(f32[]{:T(128)} %psum.14), channel_id=1, replica_groups=mesh['grp_0'=2,'grp_1'=2,'pair_0'=4,'pair_1'=2,'pair_2'=8] {'grp_1'}, use_global_device_ids=true, to_apply=%region_4.5 | all-reduce | flops 1 | bytes 8 | tf_op jit(solution)/shard_map/psum | solution.py:356
  92.7 0.6 dynamic_slice.3
  94.6 30.3 %all-to-all-done.3.operator_hbm = bf16[64,16,1024]{2,1,0:T(8,128)(2,1)} async-done(((bf16[64,16,1024]{2,1,0:T(8,128)(2,1)}), bf16[64,16,1024]{2,1,0:T(8,128)(2,1)}, u32[]{:S(2)}, u32[]{:S(2)}) %all-to-all-start.3) | async-done | bytes 2097184 | tf_op jit(solution)/shard_map/all_to_all | solution.py:326
  124.9 0.0 copy-done.1
  124.9 10.1 %step.1 = (f32[1024,512]{1,0:T(8,128)}, f32[1024,512]{1,0:T(8,128)}) custom-call(bf16[64,16,1024]{2,1,0:T(8,128)(2,1)} %all-to-all-done.3.operator_hbm, bf16[1024,512]{1,0:T(8,128)(2,1)S(1)} %copy-done, f32[1024,512]{1,0:T(8,128)S(1)} %bitcast.10), custom_call_target="tpu_custom_call" | custom-call | tf_op jit(solution)/shard_map/step/pallas_call | solution.py:308
  (5 shorter events, 0.1 us)
Async XLA Ops:
  20.0 16.7 %copy-start = (bf16[1024,512]{1,0:T(8,128)(2,1)S(1)}, bf16[1024,512]{1,0:T(8,128)(2,1)}, u32[]{:S(2)}) copy-start(bf16[1024,512]{1,0:T(8,128)(2,1)} %trial.3) | copy-start | bytes 3145732
  20.0 31.7 %all-to-all-start = ((bf16[64,16,512]{2,1,0:T(8,128)(2,1)}), bf16[64,16,512]{2,1,0:T(8,128)(2,1)S(1)}, u32[]{:S(2)}, u32[]{:S(2)}) async-start(bf16[64,16,512]{2,1,0:T(8,128)(2,1)} %bitcast.2), calls=%async_computation | async-start | bytes 2097152 | tf_op jit(solution)/shard_map/all_to_all | solution.py:326
  51.7 22.8 %copy-start.2 = (bf16[128,16384]{1,0:T(8,128)(2,1)S(1)}, bf16[128,16384]{1,0:T(8,128)(2,1)}, u32[]{:S(2)}) copy-start(bf16[128,16384]{1,0:T(8,128)(2,1)} %get-tuple-element.10.chol) | copy-start | bytes 12582916
  51.7 22.8 %copy-start.3 = (f32[64,128]{1,0:T(8,128)S(1)}, f32[64,128]{1,0:T(8,128)}, u32[]{:S(2)}) copy-start(f32[64,128]{1,0:T(8,128)} %fields.1) | copy-start | bytes 98308
  76.7 48.2 %copy-start.1 = (f32[1,1024,512]{2,1,0:T(8,128)S(1)}, f32[1,1024,512]{2,1,0:T(8,128)}, u32[]{:S(2)}) copy-start(f32[1,1024,512]{2,1,0:T(8,128)} %param.7) | copy-start | bytes 6291460
  76.7 48.2 %all-to-all-start.3 = ((bf16[64,16,1024]{2,1,0:T(8,128)(2,1)}), bf16[64,16,1024]{2,1,0:T(8,128)(2,1)}, u32[]{:S(2)}, u32[]{:S(2)}) async-start(bf16[64,16,1024]{2,1,0:T(8,128)(2,1)} %get-tuple-element.11), calls=%async_computation.3 | async-start | bytes 4194304 | tf_op jit(solution)/shard_map/all_to_all | solution.py:326

commit v4 on v3

--- a/solution.py
+++ b/solution.py
@@ -56,10 +56,17 @@
 
 def correction(inner):
     size = inner.shape[0]
+    row = lax.broadcasted_iota(jnp.int32, (128, 128), 0)
+    col = lax.broadcasted_iota(jnp.int32, (128, 128), 1)
+    on = row == col
+    diagonal = [
+        jnp.sum(jnp.where(on, inner[c : c + 128, c : c + 128], 0.0), axis=0, keepdims=True)
+        for c in range(0, size, 128)
+    ]
+    inv = 1.0 / jnp.concatenate(diagonal, axis=1)
     row = lax.broadcasted_iota(jnp.int32, (size, size), 0)
     col = lax.broadcasted_iota(jnp.int32, (size, size), 1)
     on = row == col
-    inv = 1.0 / jnp.sum(jnp.where(on, inner, 0.0), axis=0, keepdims=True)
     e1 = jnp.where(on, 1.0, 0.0) - inner * inv
     b1 = e1.astype(BF16)
     e2 = mul(b1, b1)
@@ -71,8 +78,8 @@
 
 
 def theta_kernel(turn, trial_hbm, walkers_hbm, theta, trial, walkers, idle, sems):
-    rows = walkers.shape[0] // PIECES
-    parts = [pl.ds(c * rows, rows) for c in range(PIECES)]
+    rows = walkers.shape[0] // LOADS
+    parts = [pl.ds(c * rows, rows) for c in range(LOADS)]
     copies = []
     for c, part in enumerate(parts):
         copies.append(
@@ -113,7 +120,7 @@
             VM(trial.shape, BF16),
             VM(walkers.shape, F32),
             VM((8, 128), F32),
-            pltpu.SemaphoreType.DMA((2, PIECES)),
+            pltpu.SemaphoreType.DMA((2, LOADS)),
         ],
         compiler_params=grant(24),
         name="theta",

time: 137 us -> 137 us (level)
  no operation moved by 1% of the time
where the time goes in v4:
time: 137 us; the launch traced here: 136 us
  Pallas kernels  39.4 us (29%)
  waiting for transfers between devices  38.8 us (28%)
  blocking collectives  29.8 us (22%)
  starting transfers between devices  19.4 us (14%)
  between operations  6.14 us (4%)
  other arithmetic  2.06 us (2%)
    all_to_all x2, waiting for transfers between devices, swap(): return lax.all_to_all(array, axes, split_axis=0, concat_axis=0, tiled=True)  38.8 us
    all_to_all x2, blocking collectives, swap(): return lax.all_to_all(array, axes, split_axis=0, concat_axis=0, tiled=True)  20.2 us
    pallas_call x1, Pallas kernels, theta_call(): pl.pallas_call(theta_kernel, out_shape=jax.ShapeDtypeStruct((m, n), BF16)...  19.4 us
    all_to_all x2, starting transfers between devices, swap(): return lax.all_to_all(array, axes, split_axis=0, concat_axis=0, tiled=True)  19.4 us
    pallas_call x1, Pallas kernels, step_call(): pl.pallas_call(step_kernel, out_shape=(jax.ShapeDtypeStruct(walkers.shape...  10.1 us
    psum x2, blocking collectives, per_device(): whole = lax.psum(whole, axis)  9.59 us
    pallas_call x1, Pallas kernels, ready_call(): pl.pallas_call(ready_kernel, out_shape=(pltpu.HBM((vectors, depth * width...  5.13 us
  transfers between devices with their start and end apart: 2, of which 2 were waited for; matrix products, arithmetic and copies ran while one was open for 2% of the time, Pallas kernels for 4%

profile of v4, /device:TPU:1, one launch (start us, length us, event | category | flops | bytes accessed | tf_op | source)
XLA Modules:
  0.0 136.2 jit_solution(8315447264726814075)
XLA Ops:
  0.6 19.4 %theta.1 = bf16[1024,512]{1,0:T(8,128)(2,1)} custom-call(s32[1]{0:T(128)} %bitcast.turn, bf16[1024,512]{1,0:T(8,128)(2,1)} %trial.3, f32[1024,512]{1,0:T(8,128)} %bitcast.9), custom_call_target="tpu_custom_call" | custom-call | tf_op jit(solution)/shard_map/theta/pallas_call | solution.py:114
  20.1 0.0 copy-start
  20.1 13.7 %all-to-all-start = ((bf16[64,16,512]{2,1,0:T(8,128)(2,1)}), bf16[64,16,512]{2,1,0:T(8,128)(2,1)S(1)}, u32[]{:S(2)}, u32[]{:S(2)}) async-start(bf16[64,16,512]{2,1,0:T(8,128)(2,1)} %bitcast.2), calls=%async_computation | async-start | bytes 2097152 | tf_op jit(solution)/shard_map/all_to_all | solution.py:333
  36.8 0.0 copy-done
  36.8 5.1 %ready.1 = (bf16[128,16384]{1,0:T(8,128)(2,1)}, bf16[128,8192]{1,0:T(8,128)(2,1)}) custom-call(bf16[128,16,1024]{2,1,0:T(8,128)(2,1)} %chol_hbm.1, bf16[1024,512]{1,0:T(8,128)(2,1)S(1)} %copy-done), custom_call_target="tpu_custom_call" | custom-call | tf_op jit(solution)/shard_map/ready/pallas_call | solution.py:160
  42.0 1.3 select_convert_fusion.extra
  43.3 8.5 %all-to-all-done.theta = bf16[64,16,512]{2,1,0:T(8,128)(2,1)S(1)} async-done(((bf16[64,16,512]{2,1,0:T(8,128)(2,1)}), bf16[64,16,512]{2,1,0:T(8,128)(2,1)S(1)}, u32[]{:S(2)}, u32[]{:S(2)}) %all-to-all-start) | async-done | bytes 1048608 | tf_op jit(solution)/shard_map/all_to_all | solution.py:333
  51.8 0.0 copy-start.2
  51.8 0.0 copy-start.3
  51.8 2.5 %bias.1 = bf16[8,80,128]{2,1,0:T(8,128)(2,1)S(1)} custom-call(bf16[64,16,512]{2,1,0:T(8,128)(2,1)S(1)} %all-to-all-done.theta, bf16[128,8192]{1,0:T(8,128)(2,1)} %get-tuple-element.9.met_hbm, bf16[16,128]{1,0:T(8,128)(2,1)S(1)} %select_convert_fusion.extra), custom_call_target="tpu_custom_call" | custom-call | tf_op jit(solution)/shard_map/bias/pallas_call | solution.py:202
  54.3 11.6 %all_to_all.20.parts = bf16[8,80,128]{2,1,0:T(8,128)(2,1)S(1)} all-to-all(bf16[8,80,128]{2,1,0:T(8,128)(2,1)S(1)} %bias.1), channel_id=1, replica_groups=mesh['grp_0'=2,'grp_1'=2,'pair_0'=4,'pair_1'=2,'pair_2'=8] {'pair_2'}, dimensions={0} | all-to-all | bytes 327680 | tf_op jit(solution)/shard_map/all_to_all | solution.py:333
  66.0 8.6 %all_to_all.21.parts = bf16[8,80,128]{2,1,0:T(8,128)(2,1)S(1)} all-to-all(bf16[8,80,128]{2,1,0:T(8,128)(2,1)S(1)} %spread.1), channel_id=1, replica_groups=mesh['grp_0'=2,'grp_1'=2,'pair_0'=4,'pair_1'=2,'pair_2'=8] {'pair_0','pa..., dimensions={0} | all-to-all | bytes 327680 | tf_op jit(solution)/shard_map/all_to_all | solution.py:333
  74.6 0.0 copy-done.2
  74.6 0.0 copy-done.3
  74.6 2.1 %operator.1 = (bf16[64,16,1024]{2,1,0:T(8,128)(2,1)}, f32[80,128]{1,0:T(8,128)S(1)}) custom-call(bf16[8,80,128]{2,1,0:T(8,128)(2,1)S(1)} %all_to_all.21.parts, f32[64,128]{1,0:T(8,128)S(1)} %copy-done.3, bf16[128,16384]{1,0:T(8,128)(2,1)S(1)} %copy-done.2), custom_call_target="tpu_custom_call" | custom-call | tf_op jit(solution)/shard_map/operator/pallas_call | solution.py:256
  76.7 0.0 copy-start.1
  76.7 5.7 %all-to-all-start.3 = ((bf16[64,16,1024]{2,1,0:T(8,128)(2,1)}), bf16[64,16,1024]{2,1,0:T(8,128)(2,1)}, u32[]{:S(2)}, u32[]{:S(2)}) async-start(bf16[64,16,1024]{2,1,0:T(8,128)(2,1)} %get-tuple-element.11), calls=%async_computation.3 | async-start | bytes 4194304 | tf_op jit(solution)/shard_map/all_to_all | solution.py:333
  82.5 0.1 subtract_reduce_fusion
  82.6 0.6 multiply_reduce_fusion
  83.2 6.3 %psum.14 = f32[]{:T(128)} all-reduce(f32[]{:T(128)} %get-tuple-element.15), channel_id=1, replica_groups=mesh['grp_0'=2,'grp_1'=2,'pair_0'=4,'pair_1'=2,'pair_2'=8] {'grp_0'}, use_global_device_ids=true, to_apply=%region_3.4 | all-reduce | flops 1 | bytes 8 | tf_op jit(solution)/shard_map/psum | solution.py:363
  89.5 3.3 %psum.15 = f32[]{:T(128)} all-reduce(f32[]{:T(128)} %psum.14), channel_id=1, replica_groups=mesh['grp_0'=2,'grp_1'=2,'pair_0'=4,'pair_1'=2,'pair_2'=8] {'grp_1'}, use_global_device_ids=true, to_apply=%region_4.5 | all-reduce | flops 1 | bytes 8 | tf_op jit(solution)/shard_map/psum | solution.py:363
  92.8 0.6 dynamic_slice.3
  94.7 30.3 %all-to-all-done.3.operator_hbm = bf16[64,16,1024]{2,1,0:T(8,128)(2,1)} async-done(((bf16[64,16,1024]{2,1,0:T(8,128)(2,1)}), bf16[64,16,1024]{2,1,0:T(8,128)(2,1)}, u32[]{:S(2)}, u32[]{:S(2)}) %all-to-all-start.3) | async-done | bytes 2097184 | tf_op jit(solution)/shard_map/all_to_all | solution.py:333
  125.0 0.0 copy-done.1
  125.0 10.1 %step.1 = (f32[1024,512]{1,0:T(8,128)}, f32[1024,512]{1,0:T(8,128)}) custom-call(bf16[64,16,1024]{2,1,0:T(8,128)(2,1)} %all-to-all-done.3.operator_hbm, bf16[1024,512]{1,0:T(8,128)(2,1)S(1)} %copy-done, f32[1024,512]{1,0:T(8,128)S(1)} %bitcast.10), custom_call_target="tpu_custom_call" | custom-call | tf_op jit(solution)/shard_map/step/pallas_call | solution.py:315
  (5 shorter events, 0.1 us)
Async XLA Ops:
  20.1 16.7 %copy-start = (bf16[1024,512]{1,0:T(8,128)(2,1)S(1)}, bf16[1024,512]{1,0:T(8,128)(2,1)}, u32[]{:S(2)}) copy-start(bf16[1024,512]{1,0:T(8,128)(2,1)} %trial.3) | copy-start | bytes 3145732
  20.1 31.7 %all-to-all-start = ((bf16[64,16,512]{2,1,0:T(8,128)(2,1)}), bf16[64,16,512]{2,1,0:T(8,128)(2,1)S(1)}, u32[]{:S(2)}, u32[]{:S(2)}) async-start(bf16[64,16,512]{2,1,0:T(8,128)(2,1)} %bitcast.2), calls=%async_computation | async-start | bytes 2097152 | tf_op jit(solution)/shard_map/all_to_all | solution.py:333
  51.8 22.8 %copy-start.2 = (bf16[128,16384]{1,0:T(8,128)(2,1)S(1)}, bf16[128,16384]{1,0:T(8,128)(2,1)}, u32[]{:S(2)}) copy-start(bf16[128,16384]{1,0:T(8,128)(2,1)} %get-tuple-element.10.chol) | copy-start | bytes 12582916
  51.8 22.8 %copy-start.3 = (f32[64,128]{1,0:T(8,128)S(1)}, f32[64,128]{1,0:T(8,128)}, u32[]{:S(2)}) copy-start(f32[64,128]{1,0:T(8,128)} %fields.1) | copy-start | bytes 98308
  76.7 48.2 %copy-start.1 = (f32[1,1024,512]{2,1,0:T(8,128)S(1)}, f32[1,1024,512]{2,1,0:T(8,128)}, u32[]{:S(2)}) copy-start(f32[1,1024,512]{2,1,0:T(8,128)} %param.7) | copy-start | bytes 6291460
  76.7 48.2 %all-to-all-start.3 = ((bf16[64,16,1024]{2,1,0:T(8,128)(2,1)}), bf16[64,16,1024]{2,1,0:T(8,128)(2,1)}, u32[]{:S(2)}, u32[]{:S(2)}) async-start(bf16[64,16,1024]{2,1,0:T(8,128)(2,1)} %get-tuple-element.11), calls=%async_computation.3 | async-start | bytes 4194304 | tf_op jit(solution)/shard_map/all_to_all | solution.py:333
